TPU v7x, 32 devices: a whole 2x2x4 slice. The times are simulated.
32 devices in a mesh: gx: 8 (over z, core), gy: 4 (over y, x).
Axes of the slice: x: 2, y: 2, z: 4, core: 2. Of those that a mesh axis runs over, the one named last changes fastest.
Arguments:
- velocity: float32 [2, 512, 1024], P(None, 'gy', 'gx'), may hold values from -6 to 6
- wind_stress: float32 [2, 512, 1024], P(None, 'gy', 'gx'), may hold values from -6 to 6
- thickness: float32 [512, 1024], P('gy', 'gx'), may hold values from 0.3 to 3
- ice_mask: int32 [512, 1024], P('gy', 'gx'), may hold values from 0 to 1
- land_mask: int32 [512, 1024], P('gy', 'gx'), may hold values from 0 to 1
Outputs:
- velocity_out: float32 [2, 512, 1024], P(None, 'gy', 'gx')
All inputs are finite; a program needn't handle non-finite values.
Results may differ from a plain program's by a relative error of at most 0.0012.
Values sent between devices are 32-bit elements; how exact they have to be, the bound alone decides.
A program may use at most 64 MiB of HBM per device.

v0:
```python
import functools

import jax
import jax.numpy as jnp
from jax import lax
from jax.experimental import pallas as pl
from jax.experimental.pallas import tpu as pltpu
from jax.sharding import PartitionSpec as P

PASSES = 2
CORIOLIS = 1.0
DELTA_MIN = 0.25
WIND_GAIN = 0.2
MESH = pl.DeviceIdType.MESH

XM, XP, YM, YP = 0, 1, 2, 3
AXIS = ("gx", "gx", "gy", "gy")
STEP = (-1, 1, -1, 1)


def below(array, stride, fill):
    rows = array.shape[0]
    if stride % 8 == 0:
        filler = jnp.broadcast_to(jnp.float32(fill), (stride, array.shape[1]))
        return jnp.concatenate([filler, array[:-stride]], axis=0)
    row = lax.broadcasted_iota(jnp.int32, array.shape, 0)
    return jnp.where(row < stride, fill, pltpu.roll(array, stride, 0))


def above(array, stride, fill):
    rows = array.shape[0]
    if stride % 8 == 0:
        filler = jnp.broadcast_to(jnp.float32(fill), (stride, array.shape[1]))
        return jnp.concatenate([array[stride:], filler], axis=0)
    row = lax.broadcasted_iota(jnp.int32, array.shape, 0)
    return jnp.where(row >= rows - stride, fill, pltpu.roll(array, rows - stride, 0))


def reduce_matrix(low, excess, high):
    inv = 1.0 / (excess + low + high)
    first = inv
    p, q, f = low * inv, high * inv, excess * inv
    steps = []
    stride = 1
    while stride < low.shape[0]:
        p_next = p * below(p, stride, 1.0)
        q_next = q * above(q, stride, 1.0)
        f_next = f + p * below(f, stride, 0.0) + q * above(f, stride, 0.0)
        inv = 1.0 / (f_next + p_next + q_next)
        steps.append((stride, p, q, inv))
        p, q, f = p_next * inv, q_next * inv, f_next * inv
        stride *= 2
    return first, steps, p, q, f


def reduce_right(right, first, steps):
    g = right * first
    for stride, p, q, inv in steps:
        g = (g + p * below(g, stride, 0.0) + q * above(g, stride, 0.0)) * inv
    return g


def pack_ends(g, p, q, f):
    return jnp.concatenate(
        [g[:1], p[:1], q[:1], f[:1], g[-1:], p[-1:], q[-1:], f[-1:]], axis=0
    )


def left_step(rows, state):
    g0, p0, q0, f0, g1, p1, q1, f1 = rows
    a, b, c = state
    inv = 1.0 / (f0 + q0 + p0 * c)
    head_a = (g0 + p0 * a) * inv
    head_b = q0 * inv
    head_c = (f0 + p0 * c) * inv
    new = (
        g1 + p1 * (a + b * head_a),
        q1 + p1 * (b * head_b),
        f1 + p1 * (c + b * head_c),
    )
    return new, (head_a, head_b)


def right_step(rows, state):
    g0, p0, q0, f0, g1, p1, q1, f1 = rows
    new, _ = left_step((g1, q1, p1, f1, g0, q0, p0, f0), state)
    return new


def outer_values(block_of, me, count):
    mine = block_of(me)
    zero = jnp.zeros_like(mine[0])
    left = (zero, zero, zero + 1.0)
    right = (zero, zero, zero + 1.0)
    for j in range(count - 1):
        new, _ = left_step(block_of(j), left)
        left = tuple(jnp.where(j < me, n, o) for n, o in zip(new, left))
        k = count - 1 - j
        new = right_step(block_of(k), right)
        right = tuple(jnp.where(k > me, n, o) for n, o in zip(new, right))
    (a, b, c), (head_a, head_b) = left_step(mine, left)
    ra, rb, rc = right
    last = (a + b * ra) / (c + b * rc)
    after = ra + rb * last
    before = left[0] + left[1] * (head_a + head_b * after)
    return before, after


def kernel(
    sizes,
    velocity, wind, thickness_ref, ice, land,
    out,
    halo_out, halo_in, ends_x, ends_y,
    halo_send, halo_recv, x_send, x_recv, y_send, y_recv,
):
    me = {name: lax.axis_index(name) for name in ("gx", "gy")}
    barrier = pltpu.get_barrier_semaphore()
    total = 0
    for name in ("gx", "gy"):
        for k in range(1, sizes[name]):
            pl.semaphore_signal(
                barrier,
                device_id={name: lax.rem(me[name] + k, sizes[name])},
                device_id_type=MESH,
            )
            total += 1

    def has(direction):
        name = AXIS[direction]
        if STEP[direction] < 0:
            return me[name] > 0
        return me[name] < sizes[name] - 1

    def halo_copy(slot, direction):
        return pltpu.make_async_remote_copy(
            src_ref=halo_out.at[slot, direction],
            dst_ref=halo_in.at[slot, direction ^ 1],
            send_sem=halo_send.at[slot, direction],
            recv_sem=halo_recv.at[slot, direction ^ 1],
            device_id={AXIS[direction]: me[AXIS[direction]] + STEP[direction]},
            device_id_type=MESH,
        )

    def halo_start(slot, direction, rows):
        for n, row in enumerate(rows):
            halo_out[slot, direction, n : n + 1, :] = row

        @pl.when(has(direction))
        def _():
            halo_copy(slot, direction).start()

    def halo_wait(slot, direction, count):
        @pl.when(has(direction))
        def _():
            pltpu.make_async_remote_copy(
                src_ref=halo_out.at[slot, direction],
                dst_ref=halo_in.at[slot, direction],
                send_sem=halo_send.at[slot, direction],
                recv_sem=halo_recv.at[slot, direction],
                device_id={AXIS[direction]: me[AXIS[direction]] + STEP[direction]},
                device_id_type=MESH,
            ).wait()

        block = jnp.where(has(direction), halo_in[slot, direction], 0.0)
        return [block[n : n + 1] for n in range(count)]

    def ends_copy(name, buf, sweep, send, recv, k, source):
        return pltpu.make_async_remote_copy(
            src_ref=buf.at[sweep, source],
            dst_ref=buf.at[sweep, source],
            send_sem=send.at[sweep, k - 1],
            recv_sem=recv.at[sweep, k - 1],
            device_id={name: lax.rem(me[name] + k, sizes[name])},
            device_id_type=MESH,
        )

    def gather_start(name, buf, sweep, send, recv, block):
        buf[sweep, me[name]] = block
        for k in range(1, sizes[name]):
            ends_copy(name, buf, sweep, send, recv, k, me[name]).start()

    def gather_wait(name, buf, sweep, send, recv):
        count = sizes[name]
        for k in range(1, count):
            source = lax.rem(me[name] + count - k, count)
            ends_copy(name, buf, sweep, send, recv, k, source).wait_recv()

        def block_of(j):
            block = buf[sweep, j]
            return [block[n : n + 1] for n in range(8)]

        return outer_values(block_of, me[name], count)

    def gather_finish(name, buf, sweep, send, recv):
        for k in range(1, sizes[name]):
            ends_copy(name, buf, sweep, send, recv, k, me[name]).wait_send()

    cy, cx = thickness_ref.shape
    cell_count = float(cy * cx)
    weak = 1.0 / (16.0 * cell_count)
    press = cell_count ** (-0.25)
    drive = WIND_GAIN * cell_count ** (-0.75)

    u, v = velocity[0], velocity[1]
    thickness = thickness_ref[...]
    u_t, v_t, thickness_t = u.T, v.T, thickness.T

    pl.semaphore_wait(barrier, total)
    halo_start(0, XM, (u_t[:1], v_t[:1], thickness_t[:1]))
    halo_start(0, XP, (u_t[-1:], v_t[-1:], thickness_t[-1:]))
    halo_start(0, YM, (u[:1], v[:1], thickness[:1]))
    halo_start(0, YP, (u[-1:], v[-1:], thickness[-1:]))

    active = (ice[...] * (1 - land[...])).astype(jnp.float32)
    live = active > 0.5
    live_t = active.T > 0.5
    ice_mass = weak * thickness
    wind_x = drive * wind[0]
    wind_y = drive * wind[1]

    u_xm, v_xm, p_xm = halo_wait(0, XM, 3)
    u_xp, v_xp, p_xp = halo_wait(0, XP, 3)
    u_ym, v_ym, p_ym = halo_wait(0, YM, 3)
    u_yp, v_yp, p_yp = halo_wait(0, YP, 3)
    press_x = 0.5 * press * (above(thickness_t, 1, p_xp) - below(thickness_t, 1, p_xm))
    press_y = 0.5 * press * (above(thickness, 1, p_yp) - below(thickness, 1, p_ym))

    for sweep in range(PASSES):
        if sweep:
            (v_xm,) = halo_wait(2 * sweep, XM, 1)
            (v_xp,) = halo_wait(2 * sweep, XP, 1)
            (u_ym,) = halo_wait(2 * sweep, YM, 1)
            (u_yp,) = halo_wait(2 * sweep, YP, 1)
        v_east, v_west = above(v_t, 1, v_xp), below(v_t, 1, v_xm)
        u_north, u_south = above(u, 1, u_yp), below(u, 1, u_ym)
        strain_xx = (0.5 * (above(u_t, 1, u_xp) - below(u_t, 1, u_xm))).T
        strain_yy = 0.5 * (above(v, 1, v_yp) - below(v, 1, v_ym))
        shear = 0.25 * ((u_north - u_south) + (v_east - v_west).T)
        delta2 = (
            1.25 * (strain_xx * strain_xx + strain_yy * strain_yy)
            + shear * shear
            + 1.5 * strain_xx * strain_yy
        )
        visc = thickness / (2.0 * jnp.sqrt(delta2 + DELTA_MIN * DELTA_MIN))
        slot = 2 * sweep + 1
        halo_start(slot, YM, (visc[:1],))
        halo_start(slot, YP, (visc[-1:],))
        visc_t = visc.T
        halo_start(slot, XM, (visc_t[:1],))
        halo_start(slot, XP, (visc_t[-1:],))
        (visc_ym,) = halo_wait(slot, YM, 1)
        (visc_yp,) = halo_wait(slot, YP, 1)
        north = jnp.sqrt(visc * above(visc, 1, visc_yp))
        south = jnp.sqrt(visc * below(visc, 1, visc_ym))
        (visc_xm,) = halo_wait(slot, XM, 1)
        (visc_xp,) = halo_wait(slot, XP, 1)
        east = jnp.sqrt(visc_t * above(visc_t, 1, visc_xp))
        west = jnp.sqrt(visc_t * below(visc_t, 1, visc_xm))

        excess = (ice_mass + weak * (north + south)).T
        right = (
            ice_mass * u + wind_x + CORIOLIS * ice_mass * v
            + weak * (north * u_north + south * u_south)
        ).T - press_x
        first, steps, p, q, f = reduce_matrix(
            jnp.where(live_t, west, 0.0),
            jnp.where(live_t, excess, 1.0),
            jnp.where(live_t, east, 0.0),
        )
        g = reduce_right(jnp.where(live_t, right, 0.0), first, steps)
        gather_start("gx", ends_x, sweep, x_send, x_recv, pack_ends(g, p, q, f))

        excess = ice_mass + (weak * (east + west)).T
        first, steps, p_y, q_y, f_y = reduce_matrix(
            jnp.where(live, south, 0.0),
            jnp.where(live, excess, 1.0),
            jnp.where(live, north, 0.0),
        )
        right = (
            ice_mass * v + wind_y
            + (weak * (east * v_east + west * v_west)).T
            - press_y
        )

        u_xm, u_xp = gather_wait("gx", ends_x, sweep, x_send, x_recv)
        u_t = g + p * u_xm + q * u_xp
        u = u_t.T
        if sweep + 1 < PASSES:
            halo_start(2 * sweep + 2, YM, (u[:1],))
            halo_start(2 * sweep + 2, YP, (u[-1:],))
        right = right - CORIOLIS * ice_mass * u
        g = reduce_right(jnp.where(live, right, 0.0), first, steps)
        gather_start("gy", ends_y, sweep, y_send, y_recv, pack_ends(g, p_y, q_y, f_y))
        v_ym, v_yp = gather_wait("gy", ends_y, sweep, y_send, y_recv)
        v = g + p_y * v_ym + q_y * v_yp
        if sweep + 1 < PASSES:
            v_t = v.T
            halo_start(2 * sweep + 2, XM, (v_t[:1],))
            halo_start(2 * sweep + 2, XP, (v_t[-1:],))
    out[0] = u
    out[1] = v
    for sweep in range(PASSES):
        gather_finish("gx", ends_x, sweep, x_send, x_recv)
        gather_finish("gy", ends_y, sweep, y_send, y_recv)


def on_device(sizes, velocity, wind_stress, thickness, ice_mask, land_mask):
    cy, cx = thickness.shape
    wide = max(cx, cy)
    vmem = pl.BlockSpec(memory_space=pltpu.VMEM)
    nx, ny = sizes["gx"], sizes["gy"]
    slots = 2 * PASSES
    return pl.pallas_call(
        functools.partial(kernel, sizes),
        out_shape=jax.ShapeDtypeStruct(velocity.shape, jnp.float32),
        in_specs=[vmem] * 5,
        out_specs=vmem,
        scratch_shapes=[
            pltpu.VMEM((slots, 4, 8, wide), jnp.float32),
            pltpu.VMEM((slots, 4, 8, wide), jnp.float32),
            pltpu.VMEM((PASSES, nx, 8, cy), jnp.float32),
            pltpu.VMEM((PASSES, ny, 8, cx), jnp.float32),
            pltpu.SemaphoreType.DMA((slots, 4)),
            pltpu.SemaphoreType.DMA((slots, 4)),
            pltpu.SemaphoreType.DMA((PASSES, nx - 1)),
            pltpu.SemaphoreType.DMA((PASSES, nx - 1)),
            pltpu.SemaphoreType.DMA((PASSES, ny - 1)),
            pltpu.SemaphoreType.DMA((PASSES, ny - 1)),
        ],
        compiler_params=pltpu.CompilerParams(collective_id=0, has_side_effects=True),
        name="ice_relaxation",
    )(velocity, wind_stress, thickness, ice_mask, land_mask)


def solution(mesh):
    sizes = {name: int(mesh.shape[name]) for name in ("gx", "gy")}
    cells = P("gy", "gx")
    pairs = P(None, "gy", "gx")
    return jax.shard_map(
        functools.partial(on_device, sizes),
        mesh=mesh,
        in_specs=(pairs, pairs, cells, cells, cells),
        out_specs=pairs,
        check_vma=False,
    )
```

profile of v0, /device:TPU:0, one launch (start us, length us, event | category | flops | bytes accessed | tf_op | source)
XLA Modules:
  0.0 35.9 jit_solution(15364414655565964313)
XLA Ops:
  0.0 34.3 %ice_relaxation.1 = f32[2,128,128]{2,1,0:T(8,128)} custom-call(f32[2,128,128]{2,1,0:T(8,128)} %velocity.1, f32[2,128,128]{2,1,0:T(8,128)} %wind.1, f32[128,128]{1,0:T(8,128)} %thickness_ref.1, s32[128,128]{1,0:T(8,128)} %ice.1, s32[128,128]{1,0:T(8,128)} %land.1), custom_call_target="tpu_custom_call" | custom-call | tf_op jit(solution)/shard_map/ice_relaxation/pallas_call | solution.py:313
  34.3 1.6 %copy.7 = f32[2,128,128]{2,1,0:T(8,128)} copy(f32[2,128,128]{2,1,0:T(8,128)} %ice_relaxation.1) | data formatting | bytes 262144
where the time goes:
time: 36 us; the launch traced here: 35.9 us
  Pallas kernels  34.3 us (95%)
  local copies, waits for them, and re-layouts  1.57 us (4%)
    pallas_call x1, Pallas kernels, on_device(): pl.pallas_call(functools.partial(kernel, sizes), out_shape=jax.ShapeDtype...  34.3 us
    unnamed x1, local copies, waits for them, and re-layouts  1.57 us

commit v1 on v0

v1 whole, which is shorter than its diff:
```python
import functools

import jax
import jax.numpy as jnp
from jax import lax
from jax.experimental import pallas as pl
from jax.experimental.pallas import tpu as pltpu
from jax.sharding import PartitionSpec as P

PASSES = 2
CORIOLIS = 1.0
DELTA_MIN = 0.25
WIND_GAIN = 0.2
MESH = pl.DeviceIdType.MESH

XM, XP, YM, YP = 0, 1, 2, 3
AXIS = ("gx", "gx", "gy", "gy")
STEP = (-1, 1, -1, 1)


def below(array, stride, fill):
    rows = array.shape[0]
    if stride % 8 == 0:
        filler = jnp.broadcast_to(jnp.float32(fill), (stride, array.shape[1]))
        return jnp.concatenate([filler, array[:-stride]], axis=0)
    row = lax.broadcasted_iota(jnp.int32, array.shape, 0)
    return jnp.where(row < stride, fill, pltpu.roll(array, stride, 0))


def above(array, stride, fill):
    rows = array.shape[0]
    if stride % 8 == 0:
        filler = jnp.broadcast_to(jnp.float32(fill), (stride, array.shape[1]))
        return jnp.concatenate([array[stride:], filler], axis=0)
    row = lax.broadcasted_iota(jnp.int32, array.shape, 0)
    return jnp.where(row >= rows - stride, fill, pltpu.roll(array, rows - stride, 0))


def reduce_matrix(low, excess, high):
    inv = 1.0 / (excess + low + high)
    first = inv
    p, q, f = low * inv, high * inv, excess * inv
    steps = []
    stride = 1
    while stride < low.shape[0]:
        p_next = p * below(p, stride, 1.0)
        q_next = q * above(q, stride, 1.0)
        f_next = f + p * below(f, stride, 0.0) + q * above(f, stride, 0.0)
        inv = 1.0 / (f_next + p_next + q_next)
        steps.append((stride, p, q, inv))
        p, q, f = p_next * inv, q_next * inv, f_next * inv
        stride *= 2
    return first, steps, p, q, f


def reduce_right(right, first, steps):
    g = right * first
    for stride, p, q, inv in steps:
        g = (g + p * below(g, stride, 0.0) + q * above(g, stride, 0.0)) * inv
    return g


def ends_matrix(p, q, f):
    return jnp.concatenate([p[:1], q[:1], f[:1], p[-1:], q[-1:], f[-1:]], axis=0)


def ends_right(g):
    return jnp.concatenate([g[:1], g[-1:]], axis=0)


def link(matrix, b, c):
    p0, q0, f0, p1, q1, f1 = matrix
    inv = 1.0 / (f0 + q0 + p0 * c)
    head_b = q0 * inv
    head_c = (f0 + p0 * c) * inv
    through = p1 * b * inv
    gains = (p1 + through * p0, through)
    return q1 + p1 * (b * head_b), f1 + p1 * (c + b * head_c), gains, (inv, head_b)


def chain_matrix(matrix_of, me, count):
    mine = matrix_of(me)
    zero = jnp.zeros_like(mine[0])
    lb, lc, rb, rc = zero, zero + 1.0, zero, zero + 1.0
    links = []
    for j in range(count - 1):
        nb, nc, gains, _ = link(matrix_of(j), lb, lc)
        take = j < me
        lb, lc = jnp.where(take, nb, lb), jnp.where(take, nc, lc)
        k = count - 1 - j
        p0, q0, f0, p1, q1, f1 = matrix_of(k)
        nb, nc, back, _ = link((q1, p1, f1, q0, p0, f0), rb, rc)
        take = k > me
        rb, rc = jnp.where(take, nb, rb), jnp.where(take, nc, rc)
        links.append((gains, back))
    b, c, gains, (inv, head_b) = link(mine, lb, lc)
    last_inv = 1.0 / (c + b * rc)
    return links, gains, mine[0] * inv, inv, head_b, lb, b, rb, last_inv


def chain_right(right_of, chain, me, count):
    links, gains, p0_inv, inv, head_b, left_b, b, rb, last_inv = chain
    mine = right_of(me)
    left = right = jnp.zeros_like(mine[0])
    for j, (ahead, back) in enumerate(links):
        g0, g1 = right_of(j)
        left = jnp.where(j < me, g1 + ahead[0] * left + ahead[1] * g0, left)
        k = count - 1 - j
        g0, g1 = right_of(k)
        right = jnp.where(k > me, g0 + back[0] * right + back[1] * g1, right)
    a = mine[1] + gains[0] * left + gains[1] * mine[0]
    last = (a + b * right) * last_inv
    after = right + rb * last
    before = left + left_b * (mine[0] * inv + p0_inv * left + head_b * after)
    return before, after


def lane_below(row, corner):
    lane = lax.broadcasted_iota(jnp.int32, row.shape, 1)
    return jnp.where(lane == 0, corner, pltpu.roll(row, 1, 1))


def lane_above(row, corner):
    lane = lax.broadcasted_iota(jnp.int32, row.shape, 1)
    return jnp.where(
        lane == row.shape[1] - 1, corner, pltpu.roll(row, row.shape[1] - 1, 1)
    )


def viscosity_of(strain_xx, strain_yy, shear, thickness):
    delta2 = (
        1.25 * (strain_xx * strain_xx + strain_yy * strain_yy)
        + shear * shear
        + 1.5 * strain_xx * strain_yy
    )
    return thickness / (2.0 * jnp.sqrt(delta2 + DELTA_MIN * DELTA_MIN))


def kernel(
    sizes,
    velocity_hbm, wind_hbm, thickness_hbm, ice_hbm, land_hbm,
    out,
    velocity, wind, thickness_ref, ice, land, in_sem,
    halo_out, halo_in, diag_out, diag_in,
    x_matrix, x_right, y_matrix, y_right, y_steps, y_rest,
    halo_send, halo_recv, diag_send, diag_recv,
    xm_send, xm_recv, xr_send, xr_recv, ym_send, ym_recv, yr_send, yr_recv,
):
    me = {name: lax.axis_index(name) for name in ("gx", "gy")}
    loads = [
        pltpu.make_async_copy(src, dst, in_sem.at[n])
        for n, (src, dst) in enumerate(
            (
                (velocity_hbm, velocity), (thickness_hbm, thickness_ref),
                (wind_hbm, wind), (ice_hbm, ice), (land_hbm, land),
            )
        )
    ]
    for load in loads:
        load.start()

    def has(direction):
        name = AXIS[direction]
        if STEP[direction] < 0:
            return me[name] > 0
        return me[name] < sizes[name] - 1

    corners = [(x, y) for x in (XM, XP) for y in (YM, YP)]

    def corner_id(x, y):
        return {"gx": me["gx"] + STEP[x], "gy": me["gy"] + STEP[y]}

    def has_corner(x, y):
        return jnp.logical_and(has(x), has(y))

    barrier = pltpu.get_barrier_semaphore()
    total = 0
    for name in ("gx", "gy"):
        for k in range(1, sizes[name]):
            pl.semaphore_signal(
                barrier,
                device_id={name: lax.rem(me[name] + k, sizes[name])},
                device_id_type=MESH,
            )
            total += 1
    for x, y in corners:
        total = total + jnp.where(has_corner(x, y), 1, 0)

        @pl.when(has_corner(x, y))
        def _():
            pl.semaphore_signal(
                barrier, device_id=corner_id(x, y), device_id_type=MESH
            )

    def halo_copy(slot, direction, landing):
        return pltpu.make_async_remote_copy(
            src_ref=halo_out.at[slot, direction],
            dst_ref=halo_in.at[slot, landing],
            send_sem=halo_send.at[slot, direction],
            recv_sem=halo_recv.at[slot, landing],
            device_id={AXIS[direction]: me[AXIS[direction]] + STEP[direction]},
            device_id_type=MESH,
        )

    def halo_fill(slot, direction, rows):
        for n, row in enumerate(rows):
            halo_out[slot, direction, n : n + 1, : row.shape[1]] = row

    def halo_start(slot, direction):
        @pl.when(has(direction))
        def _():
            halo_copy(slot, direction, direction ^ 1).start()

    def halo_wait(slot, direction, count):
        @pl.when(has(direction))
        def _():
            halo_copy(slot, direction, direction).wait()

        wide = cy if AXIS[direction] == "gx" else cx
        block = jnp.where(has(direction), halo_in[slot, direction, :, :wide], 0.0)
        return [block[n : n + 1] for n in range(count)]

    def diag_copy(n, landing):
        return pltpu.make_async_remote_copy(
            src_ref=diag_out.at[n],
            dst_ref=diag_in.at[landing],
            send_sem=diag_send.at[n],
            recv_sem=diag_recv.at[landing],
            device_id=corner_id(*corners[n]),
            device_id_type=MESH,
        )

    def ends_copy(name, ends, sweep, k, source):
        buf, send, recv = ends
        return pltpu.make_async_remote_copy(
            src_ref=buf.at[sweep, source],
            dst_ref=buf.at[sweep, source],
            send_sem=send.at[sweep, k - 1],
            recv_sem=recv.at[sweep, k - 1],
            device_id={name: lax.rem(me[name] + k, sizes[name])},
            device_id_type=MESH,
        )

    def gather_start(name, ends, sweep, block):
        ends[0][sweep, me[name]] = block
        for k in range(1, sizes[name]):
            ends_copy(name, ends, sweep, k, me[name]).start()

    def gather_wait(name, ends, sweep):
        count = sizes[name]
        for k in range(1, count):
            source = lax.rem(me[name] + count - k, count)
            ends_copy(name, ends, sweep, k, source).wait_recv()

        def block_of(j):
            block = ends[0][sweep, j]
            return [block[n : n + 1] for n in range(block.shape[0])]

        return block_of

    def outer_values(name, matrix, right, sweep):
        chain = chain_matrix(gather_wait(name, matrix, sweep), me[name], sizes[name])
        return chain_right(
            gather_wait(name, right, sweep), chain, me[name], sizes[name]
        )

    gathers = (
        ("gx", (x_matrix, xm_send, xm_recv)),
        ("gx", (x_right, xr_send, xr_recv)),
        ("gy", (y_matrix, ym_send, ym_recv)),
        ("gy", (y_right, yr_send, yr_recv)),
    )
    x_ends = (gathers[0][1], gathers[1][1])
    y_ends = (gathers[2][1], gathers[3][1])

    cy, cx = thickness_ref.shape
    cell_count = float(cy * cx)
    weak = 1.0 / (16.0 * cell_count)
    press = cell_count ** (-0.25)
    drive = WIND_GAIN * cell_count ** (-0.75)

    loads[0].wait()
    loads[1].wait()
    u, v = velocity[0], velocity[1]
    thickness = thickness_ref[...]
    u_t, v_t, thickness_t = u.T, v.T, thickness.T
    halo_fill(0, YM, (u[:1], v[:1], u[1:2], v[1:2], thickness[:1]))
    halo_fill(0, YP, (u[-1:], v[-1:], u[-2:-1], v[-2:-1], thickness[-1:]))
    for n, (x, y) in enumerate(corners):
        row = slice(0, 1) if y == YM else slice(cy - 1, cy)
        lane = slice(0, 1) if x == XM else slice(cx - 1, cx)
        for m, field in enumerate((u, v)):
            diag_out[n, m : m + 1, :] = jnp.broadcast_to(
                field[row, lane], (1, diag_out.shape[2])
            )
    halo_fill(0, XM, (u_t[:1], v_t[:1], u_t[1:2], v_t[1:2], thickness_t[:1]))
    halo_fill(0, XP, (u_t[-1:], v_t[-1:], u_t[-2:-1], v_t[-2:-1], thickness_t[-1:]))
    pl.semaphore_wait(barrier, total)
    for n in range(4):

        @pl.when(has_corner(*corners[n]))
        def _():
            diag_copy(n, 3 - n).start()

    for direction in (YM, YP, XM, XP):
        halo_start(0, direction)

    for load in loads[2:]:
        load.wait()
    active = (ice[...] * (1 - land[...])).astype(jnp.float32)
    live = active > 0.5
    live_t = active.T > 0.5
    ice_mass = weak * thickness
    wind_x = drive * wind[0]
    wind_y = drive * wind[1]

    for sweep in range(PASSES):
        if sweep == 0:
            u_xm, v_xm, u_xm2, v_xm2, p_xm = halo_wait(0, XM, 5)
            u_xp, v_xp, u_xp2, v_xp2, p_xp = halo_wait(0, XP, 5)
            u_ym, v_ym, u_ym2, v_ym2, p_ym = halo_wait(0, YM, 5)
            u_yp, v_yp, u_yp2, v_yp2, p_yp = halo_wait(0, YP, 5)
            corner = []
            for n in range(4):

                @pl.when(has_corner(*corners[n]))
                def _():
                    diag_copy(n, n).wait()

                block = jnp.where(has_corner(*corners[n]), diag_in[n], 0.0)
                corner.append([block[:1], block[1:2]])
            mm, mp, pm, pp = corner
            press_x = 0.5 * press * (
                above(thickness_t, 1, p_xp) - below(thickness_t, 1, p_xm)
            )
            press_y = 0.5 * press * (
                above(thickness, 1, p_yp) - below(thickness, 1, p_ym)
            )
        else:
            late = 2 * sweep
            u_xm, v_xm, u_xm2, v_xm2, *low = halo_wait(late, XM, 8)
            u_xp, v_xp, u_xp2, v_xp2, *high = halo_wait(late, XP, 8)
            mm, mp, pm, pp = low[:2], low[2:], high[:2], high[2:]
            (v_ym2,) = halo_wait(late, YM, 1)
            (v_yp2,) = halo_wait(late, YP, 1)

        v_east, v_west = above(v_t, 1, v_xp), below(v_t, 1, v_xm)
        u_north, u_south = above(u, 1, u_yp), below(u, 1, u_ym)
        strain_xx = (0.5 * (above(u_t, 1, u_xp) - below(u_t, 1, u_xm))).T
        strain_yy = 0.5 * (above(v, 1, v_yp) - below(v, 1, v_ym))
        shear = 0.25 * ((u_north - u_south) + (v_east - v_west).T)
        visc = viscosity_of(strain_xx, strain_yy, shear, thickness)

        def rim(near, minus1, minus2, plus1, plus2, m_lo, m_hi, p_lo, p_hi):
            across = jnp.concatenate([near[:1] - minus2, plus2 - near[-1:]], axis=0)
            n = minus1.shape[1]
            along = jnp.concatenate(
                [
                    lane_above(minus1, m_hi[:, :n]) - lane_below(minus1, m_lo[:, :n]),
                    lane_above(plus1, p_hi[:, :n]) - lane_below(plus1, p_lo[:, :n]),
                ],
                axis=0,
            )
            return across, along

        u_across, u_along = rim(
            u_t, u_xm, u_xm2, u_xp, u_xp2, mm[0], mp[0], pm[0], pp[0]
        )
        v_across, v_along = rim(
            v_t, v_xm, v_xm2, v_xp, v_xp2, mm[1], mp[1], pm[1], pp[1]
        )
        visc_x = viscosity_of(
            0.5 * u_across, 0.5 * v_along, 0.25 * (u_along + v_across),
            jnp.concatenate([p_xm, p_xp], axis=0),
        )
        u_across, u_along = rim(
            u, u_ym, u_ym2, u_yp, u_yp2, mm[0], pm[0], mp[0], pp[0]
        )
        v_across, v_along = rim(
            v, v_ym, v_ym2, v_yp, v_yp2, mm[1], pm[1], mp[1], pp[1]
        )
        visc_y = viscosity_of(
            0.5 * u_along, 0.5 * v_across, 0.25 * (u_across + v_along),
            jnp.concatenate([p_ym, p_yp], axis=0),
        )

        visc_t = visc.T
        north = jnp.sqrt(visc * above(visc, 1, visc_y[1:]))
        south = jnp.sqrt(visc * below(visc, 1, visc_y[:1]))
        east = jnp.sqrt(visc_t * above(visc_t, 1, visc_x[1:]))
        west = jnp.sqrt(visc_t * below(visc_t, 1, visc_x[:1]))

        excess = (ice_mass + weak * (north + south)).T
        right = (
            ice_mass * u + wind_x + CORIOLIS * ice_mass * v
            + weak * (north * u_north + south * u_south)
        ).T - press_x
        first, steps, p, q, f = reduce_matrix(
            jnp.where(live_t, west, 0.0),
            jnp.where(live_t, excess, 1.0),
            jnp.where(live_t, east, 0.0),
        )
        gather_start("gx", x_ends[0], sweep, ends_matrix(p, q, f))
        g = reduce_right(jnp.where(live_t, right, 0.0), first, steps)
        gather_start("gx", x_ends[1], sweep, ends_right(g))

        @pl.when(me["gx"] >= 0)
        def _():
            excess = ice_mass + (weak * (east + west)).T
            first, steps, p_y, q_y, f_y = reduce_matrix(
                jnp.where(live, south, 0.0),
                jnp.where(live, excess, 1.0),
                jnp.where(live, north, 0.0),
            )
            gather_start("gy", y_ends[0], sweep, ends_matrix(p_y, q_y, f_y))
            for n, (_, p_n, q_n, inv) in enumerate(steps):
                y_steps[n, 0], y_steps[n, 1], y_steps[n, 2] = p_n, q_n, inv
            right = (
                ice_mass * v + wind_y
                + (weak * (east * v_east + west * v_west)).T
                - press_y
            )
            y_rest[0], y_rest[1], y_rest[2], y_rest[3] = first, p_y, q_y, right

        u_xm, u_xp = outer_values("gx", *x_ends, sweep)
        u_t = g + p * u_xm + q * u_xp
        u = u_t.T
        if sweep + 1 < PASSES:
            early = 2 * sweep + 1
            halo_fill(early, YM, (u[:1], u[1:2]))
            halo_fill(early, YP, (u[-1:], u[-2:-1]))
            halo_start(early, YM)
            halo_start(early, YP)
        else:
            out[0] = u
        y_strides = [
            (2**n, y_steps[n, 0], y_steps[n, 1], y_steps[n, 2])
            for n in range(y_steps.shape[0])
        ]
        right = y_rest[3] - CORIOLIS * ice_mass * u
        g = reduce_right(jnp.where(live, right, 0.0), y_rest[0], y_strides)
        gather_start("gy", y_ends[1], sweep, ends_right(g))
        v_ym, v_yp = outer_values("gy", *y_ends, sweep)
        v = g + y_rest[1] * v_ym + y_rest[2] * v_yp
        if sweep + 1 < PASSES:
            late = early + 1
            halo_fill(late, YM, (v[1:2],))
            halo_fill(late, YP, (v[-2:-1],))
            halo_start(late, YM)
            halo_start(late, YP)
            u_ym, u_ym2 = halo_wait(early, YM, 2)
            u_yp, u_yp2 = halo_wait(early, YP, 2)
            v_t = v.T
            for direction, near, next_, lane in ((XM, 0, 1, 0), (XP, cx - 1, cx - 2, cx - 1)):
                rows = [
                    u_t[near : near + 1], v_t[near : near + 1],
                    u_t[next_ : next_ + 1], v_t[next_ : next_ + 1],
                ] + [
                    jnp.broadcast_to(row[:, lane : lane + 1], (1, halo_out.shape[3]))
                    for row in (u_ym, v_ym, u_yp, v_yp)
                ]
                halo_fill(late, direction, rows)
                halo_start(late, direction)
    out[1] = v
    for sweep in range(PASSES):
        for name, ends in gathers:
            for k in range(1, sizes[name]):
                ends_copy(name, ends, sweep, k, me[name]).wait_send()


def on_device(sizes, velocity, wind_stress, thickness, ice_mask, land_mask):
    cy, cx = thickness.shape
    wide = max(cx, cy)
    nx, ny = sizes["gx"], sizes["gy"]
    slots = 2 * PASSES - 1
    dma = pltpu.SemaphoreType.DMA
    strides = (cy - 1).bit_length()
    f32 = jnp.float32
    args = (velocity, wind_stress, thickness, ice_mask, land_mask)
    return pl.pallas_call(
        functools.partial(kernel, sizes),
        out_shape=jax.ShapeDtypeStruct(velocity.shape, f32),
        in_specs=[pl.BlockSpec(memory_space=pl.ANY)] * 5,
        out_specs=pl.BlockSpec(memory_space=pltpu.VMEM),
        scratch_shapes=[pltpu.VMEM(arg.shape, arg.dtype) for arg in args]
        + [
            dma((5,)),
            pltpu.VMEM((slots, 4, 8, wide), f32),
            pltpu.VMEM((slots, 4, 8, wide), f32),
            pltpu.VMEM((4, 2, wide), f32),
            pltpu.VMEM((4, 2, wide), f32),
            pltpu.VMEM((PASSES, nx, 6, cy), f32),
            pltpu.VMEM((PASSES, nx, 2, cy), f32),
            pltpu.VMEM((PASSES, ny, 6, cx), f32),
            pltpu.VMEM((PASSES, ny, 2, cx), f32),
            pltpu.VMEM((strides, 3, cy, cx), f32),
            pltpu.VMEM((4, cy, cx), f32),
            dma((slots, 4)), dma((slots, 4)), dma((4,)), dma((4,)),
        ]
        + [dma((PASSES, nx - 1))] * 4
        + [dma((PASSES, ny - 1))] * 4,
        compiler_params=pltpu.CompilerParams(collective_id=0, has_side_effects=True),
        name="ice_relaxation",
    )(*args)


def solution(mesh):
    sizes = {name: int(mesh.shape[name]) for name in ("gx", "gy")}
    cells = P("gy", "gx")
    pairs = P(None, "gy", "gx")
    return jax.shard_map(
        functools.partial(on_device, sizes),
        mesh=mesh,
        in_specs=(pairs, pairs, cells, cells, cells),
        out_specs=pairs,
        check_vma=False,
    )
```

time: 36 us -> 30.2 us (0.84)
  Pallas kernels: 34.3 us -> 28.5 us
    pallas_call x1, Pallas kernels: 34.3 us -> 28.5 us  [on_device(): pl.pallas_call(functools.partial(kernel, sizes), out_shape=jax.ShapeDtype...]
where the time goes in v1:
time: 30.2 us; the launch traced here: 30.1 us
  Pallas kernels  28.5 us (94%)
  local copies, waits for them, and re-layouts  1.57 us (5%)
    pallas_call x1, Pallas kernels, on_device(): pl.pallas_call(functools.partial(kernel, sizes), out_shape=jax.ShapeDtype...  28.5 us
    unnamed x1, local copies, waits for them, and re-layouts  1.57 us

profile of v1, /device:TPU:0, one launch (start us, length us, event | category | flops | bytes accessed | tf_op | source)
XLA Modules:
  0.0 30.1 jit_solution(13369130576705067699)
XLA Ops:
  0.0 28.5 %ice_relaxation.1 = f32[2,128,128]{2,1,0:T(8,128)} custom-call(f32[2,128,128]{2,1,0:T(8,128)} %velocity_hbm.1, f32[2,128,128]{2,1,0:T(8,128)} %wind_hbm.1, f32[128,128]{1,0:T(8,128)} %thickness_hbm.1, s32[128,128]{1,0:T(8,128)} %ice_hbm.1, s32[128,128]{1,0:T(8,128)} %land_hbm.1), custom_call_target="tpu_custom_call" | custom-call | tf_op jit(solution)/shard_map/ice_relaxation/pallas_call | solution.py:480
  28.5 1.6 %copy.7 = f32[2,128,128]{2,1,0:T(8,128)} copy(f32[2,128,128]{2,1,0:T(8,128)} %ice_relaxation.1) | data formatting | bytes 262144

commit v2 on v1

--- a/solution.py
+++ b/solution.py
@@ -479,7 +479,7 @@
     args = (velocity, wind_stress, thickness, ice_mask, land_mask)
     return pl.pallas_call(
         functools.partial(kernel, sizes),
-        out_shape=jax.ShapeDtypeStruct(velocity.shape, f32),
+        out_shape=pltpu.VMEM(velocity.shape, f32),
         in_specs=[pl.BlockSpec(memory_space=pl.ANY)] * 5,
         out_specs=pl.BlockSpec(memory_space=pltpu.VMEM),
         scratch_shapes=[pltpu.VMEM(arg.shape, arg.dtype) for arg in args]

time: 30.2 us -> 28.7 us (0.950)
  local copies, waits for them, and re-layouts: 1.57 us -> 0.66 us
  Pallas kernels: 28.5 us -> 27.9 us
    unnamed x1, local copies, waits for them, and re-layouts: 1.57 us -> 0.66 us
    pallas_call x1, Pallas kernels: 28.5 us -> 27.9 us  [on_device(): pl.pallas_call(functools.partial(kernel, sizes), out_shape=pltpu.VMEM(vel...]
where the time goes in v2:
time: 28.7 us; the launch traced here: 28.5 us
  Pallas kernels  27.9 us (97%)
  local copies, waits for them, and re-layouts  0.66 us (2%)
    pallas_call x1, Pallas kernels, on_device(): pl.pallas_call(functools.partial(kernel, sizes), out_shape=pltpu.VMEM(vel...  27.9 us
    unnamed x1, local copies, waits for them, and re-layouts  0.66 us

profile of v2, /device:TPU:0, one launch (start us, length us, event | category | flops | bytes accessed | tf_op | source)
XLA Modules:
  0.0 28.5 jit_solution(14123428241346643274)
XLA Ops:
  0.0 27.9 %ice_relaxation.1 = f32[2,128,128]{2,1,0:T(8,128)S(1)} custom-call(f32[2,128,128]{2,1,0:T(8,128)} %velocity_hbm.1, f32[2,128,128]{2,1,0:T(8,128)} %wind_hbm.1, f32[128,128]{1,0:T(8,128)} %thickness_hbm.1, s32[128,128]{1,0:T(8,128)} %ice_hbm.1, s32[128,128]{1,0:T(8,128)} %land_hbm.1), custom_call_target="tpu_custom_call" | custom-call | tf_op jit(solution)/shard_map/ice_relaxation/pallas_call | solution.py:480
  27.9 0.7 %copy.7 = f32[2,128,128]{2,1,0:T(8,128)} copy(f32[2,128,128]{2,1,0:T(8,128)S(1)} %ice_relaxation.1) | data formatting | bytes 262144

commit v3 on v2

--- a/solution.py
+++ b/solution.py
@@ -83,36 +83,50 @@
     zero = jnp.zeros_like(mine[0])
     lb, lc, rb, rc = zero, zero + 1.0, zero, zero + 1.0
     links = []
+    beyond = [(zero,) * 4] * 2
     for j in range(count - 1):
-        nb, nc, gains, _ = link(matrix_of(j), lb, lc)
+        ends = matrix_of(j)
+        nb, nc, gains, (inv, head_b) = link(ends, lb, lc)
+        keep = (lb, inv, head_b, ends[0] * inv)
+        beyond[0] = [jnp.where(j == me - 1, n, o) for n, o in zip(keep, beyond[0])]
         take = j < me
         lb, lc = jnp.where(take, nb, lb), jnp.where(take, nc, lc)
         k = count - 1 - j
         p0, q0, f0, p1, q1, f1 = matrix_of(k)
-        nb, nc, back, _ = link((q1, p1, f1, q0, p0, f0), rb, rc)
+        nb, nc, back, (inv, head_b) = link((q1, p1, f1, q0, p0, f0), rb, rc)
+        keep = (rb, inv, head_b, q1 * inv)
+        beyond[1] = [jnp.where(k == me + 1, n, o) for n, o in zip(keep, beyond[1])]
         take = k > me
         rb, rc = jnp.where(take, nb, rb), jnp.where(take, nc, rc)
         links.append((gains, back))
     b, c, gains, (inv, head_b) = link(mine, lb, lc)
     last_inv = 1.0 / (c + b * rc)
-    return links, gains, mine[0] * inv, inv, head_b, lb, b, rb, last_inv
+    return links, beyond, gains, mine[0] * inv, inv, head_b, lb, b, rb, last_inv
 
 
 def chain_right(right_of, chain, me, count):
-    links, gains, p0_inv, inv, head_b, left_b, b, rb, last_inv = chain
+    links, beyond, gains, p0_inv, inv, head_b, left_b, b, rb, last_inv = chain
     mine = right_of(me)
     left = right = jnp.zeros_like(mine[0])
+    kept = [(left, left), (left, left)]
     for j, (ahead, back) in enumerate(links):
         g0, g1 = right_of(j)
+        kept[0] = [jnp.where(j == me - 1, n, o) for n, o in zip((left, g0), kept[0])]
         left = jnp.where(j < me, g1 + ahead[0] * left + ahead[1] * g0, left)
         k = count - 1 - j
         g0, g1 = right_of(k)
+        kept[1] = [jnp.where(k == me + 1, n, o) for n, o in zip((right, g1), kept[1])]
         right = jnp.where(k > me, g0 + back[0] * right + back[1] * g1, right)
     a = mine[1] + gains[0] * left + gains[1] * mine[0]
     last = (a + b * right) * last_inv
     after = right + rb * last
-    before = left + left_b * (mine[0] * inv + p0_inv * left + head_b * after)
-    return before, after
+    first = mine[0] * inv + p0_inv * left + head_b * after
+    before = left + left_b * first
+    far = [
+        a_n + b_n * (g_n * inv_n + p_n * a_n + h_n * own)
+        for (a_n, g_n), (b_n, inv_n, h_n, p_n), own in zip(kept, beyond, (first, last))
+    ]
+    return before, after, far
 
 
 def lane_below(row, corner):
@@ -145,6 +159,7 @@
     x_matrix, x_right, y_matrix, y_right, y_steps, y_rest,
     halo_send, halo_recv, diag_send, diag_recv,
     xm_send, xm_recv, xr_send, xr_recv, ym_send, ym_recv, yr_send, yr_recv,
+    sm_send, sm_recv, sr_send, sr_recv,
 ):
     me = {name: lax.axis_index(name) for name in ("gx", "gy")}
     loads = [
@@ -173,6 +188,12 @@
     def has_corner(x, y):
         return jnp.logical_and(has(x), has(y))
 
+    def side_id(side, k):
+        return {
+            "gx": me["gx"] + STEP[side],
+            "gy": lax.rem(me["gy"] + k, sizes["gy"]),
+        }
+
     barrier = pltpu.get_barrier_semaphore()
     total = 0
     for name in ("gx", "gy"):
@@ -183,14 +204,15 @@
                 device_id_type=MESH,
             )
             total += 1
-    for x, y in corners:
-        total = total + jnp.where(has_corner(x, y), 1, 0)
-
-        @pl.when(has_corner(x, y))
+    for side in (XM, XP):
+        total = total + jnp.where(has(side), sizes["gy"] - 1, 0)
+
+        @pl.when(has(side))
         def _():
-            pl.semaphore_signal(
-                barrier, device_id=corner_id(x, y), device_id_type=MESH
-            )
+            for k in range(1, sizes["gy"]):
+                pl.semaphore_signal(
+                    barrier, device_id=side_id(side, k), device_id_type=MESH
+                )
 
     def halo_copy(slot, direction, landing):
         return pltpu.make_async_remote_copy(
@@ -202,8 +224,8 @@
             device_id_type=MESH,
         )
 
-    def halo_fill(slot, direction, rows):
-        for n, row in enumerate(rows):
+    def halo_fill(slot, direction, rows, start=0):
+        for n, row in enumerate(rows, start):
             halo_out[slot, direction, n : n + 1, : row.shape[1]] = row
 
     def halo_start(slot, direction):
@@ -233,35 +255,70 @@
     def ends_copy(name, ends, sweep, k, source):
         buf, send, recv = ends
         return pltpu.make_async_remote_copy(
-            src_ref=buf.at[sweep, source],
-            dst_ref=buf.at[sweep, source],
+            src_ref=buf.at[sweep, source, 0],
+            dst_ref=buf.at[sweep, source, 0],
             send_sem=send.at[sweep, k - 1],
             recv_sem=recv.at[sweep, k - 1],
             device_id={name: lax.rem(me[name] + k, sizes[name])},
             device_id_type=MESH,
         )
 
-    def gather_start(name, ends, sweep, block):
-        ends[0][sweep, me[name]] = block
+    def side_copy(ends, sides, sweep, side, k, source, landing):
+        buf, (send, recv) = ends[0], sides
+        return pltpu.make_async_remote_copy(
+            src_ref=buf.at[sweep, source, 0],
+            dst_ref=buf.at[sweep, source, 1 + landing],
+            send_sem=send.at[sweep, side, k],
+            recv_sem=recv.at[sweep, landing, k],
+            device_id=side_id(side, k),
+            device_id_type=MESH,
+        )
+
+    def gather_start(name, ends, sweep, block, sides=None):
+        ends[0][sweep, me[name], 0] = block
         for k in range(1, sizes[name]):
             ends_copy(name, ends, sweep, k, me[name]).start()
-
-    def gather_wait(name, ends, sweep):
+        if sides is not None:
+            for side in (XM, XP):
+
+                @pl.when(has(side))
+                def _():
+                    for k in range(sizes["gy"]):
+                        side_copy(
+                            ends, sides, sweep, side, k, me["gy"], side ^ 1
+                        ).start()
+
+    def gather_wait(name, ends, sweep, sides=None):
         count = sizes[name]
         for k in range(1, count):
             source = lax.rem(me[name] + count - k, count)
             ends_copy(name, ends, sweep, k, source).wait_recv()
+        if sides is not None:
+            for side in (XM, XP):
+
+                @pl.when(has(side))
+                def _():
+                    for k in range(count):
+                        source = lax.rem(me[name] + count - k, count)
+                        side_copy(
+                            ends, sides, sweep, side, k, source, side
+                        ).wait_recv()
 
         def block_of(j):
-            block = ends[0][sweep, j]
-            return [block[n : n + 1] for n in range(block.shape[0])]
+            blocks = [ends[0][sweep, j, n] for n in range(1 if sides is None else 3)]
+            return [
+                jnp.concatenate([block[n : n + 1] for block in blocks], axis=0)
+                for n in range(blocks[0].shape[0])
+            ]
 
         return block_of
 
-    def outer_values(name, matrix, right, sweep):
-        chain = chain_matrix(gather_wait(name, matrix, sweep), me[name], sizes[name])
+    def outer_values(name, matrix, right, sweep, sides=(None, None)):
+        chain = chain_matrix(
+            gather_wait(name, matrix, sweep, sides[0]), me[name], sizes[name]
+        )
         return chain_right(
-            gather_wait(name, right, sweep), chain, me[name], sizes[name]
+            gather_wait(name, right, sweep, sides[1]), chain, me[name], sizes[name]
         )
 
     gathers = (
@@ -273,6 +330,7 @@
     x_ends = (gathers[0][1], gathers[1][1])
     y_ends = (gathers[2][1], gathers[3][1])
 
+    side_sems = ((sm_send, sm_recv), (sr_send, sr_recv))
     cy, cx = thickness_ref.shape
     cell_count = float(cy * cx)
     weak = 1.0 / (16.0 * cell_count)
@@ -315,6 +373,9 @@
     wind_y = drive * wind[1]
 
     for sweep in range(PASSES):
+        more = sweep + 1 < PASSES
+        early, late = 2 * sweep + 1, 2 * sweep + 2
+        sides = side_sems if more else (None, None)
         if sweep == 0:
             u_xm, v_xm, u_xm2, v_xm2, p_xm = halo_wait(0, XM, 5)
             u_xp, v_xp, u_xp2, v_xp2, p_xp = halo_wait(0, XP, 5)
@@ -336,13 +397,6 @@
             press_y = 0.5 * press * (
                 above(thickness, 1, p_yp) - below(thickness, 1, p_ym)
             )
-        else:
-            late = 2 * sweep
-            u_xm, v_xm, u_xm2, v_xm2, *low = halo_wait(late, XM, 8)
-            u_xp, v_xp, u_xp2, v_xp2, *high = halo_wait(late, XP, 8)
-            mm, mp, pm, pp = low[:2], low[2:], high[:2], high[2:]
-            (v_ym2,) = halo_wait(late, YM, 1)
-            (v_yp2,) = halo_wait(late, YP, 1)
 
         v_east, v_west = above(v_t, 1, v_xp), below(v_t, 1, v_xm)
         u_north, u_south = above(u, 1, u_yp), below(u, 1, u_ym)
@@ -412,7 +466,7 @@
                 jnp.where(live, excess, 1.0),
                 jnp.where(live, north, 0.0),
             )
-            gather_start("gy", y_ends[0], sweep, ends_matrix(p_y, q_y, f_y))
+            gather_start("gy", y_ends[0], sweep, ends_matrix(p_y, q_y, f_y), sides[0])
             for n, (_, p_n, q_n, inv) in enumerate(steps):
                 y_steps[n, 0], y_steps[n, 1], y_steps[n, 2] = p_n, q_n, inv
             right = (
@@ -421,51 +475,89 @@
                 - press_y
             )
             y_rest[0], y_rest[1], y_rest[2], y_rest[3] = first, p_y, q_y, right
-
-        u_xm, u_xp = outer_values("gx", *x_ends, sweep)
+            if more:
+                p_t, q_t = p_y.T, q_y.T
+                halo_fill(late, XM, (p_t[:1], q_t[:1], p_t[1:2], q_t[1:2]))
+                halo_fill(late, XP, (p_t[-1:], q_t[-1:], p_t[-2:-1], q_t[-2:-1]))
+                halo_fill(late, YM, (p_y[1:2], q_y[1:2]))
+                halo_fill(late, YP, (p_y[-2:-1], q_y[-2:-1]))
+
+        u_xm, u_xp, _ = outer_values("gx", *x_ends, sweep)
         u_t = g + p * u_xm + q * u_xp
         u = u_t.T
-        if sweep + 1 < PASSES:
-            early = 2 * sweep + 1
-            halo_fill(early, YM, (u[:1], u[1:2]))
-            halo_fill(early, YP, (u[-1:], u[-2:-1]))
-            halo_start(early, YM)
-            halo_start(early, YP)
-        else:
-            out[0] = u
         y_strides = [
             (2**n, y_steps[n, 0], y_steps[n, 1], y_steps[n, 2])
             for n in range(y_steps.shape[0])
         ]
         right = y_rest[3] - CORIOLIS * ice_mass * u
         g = reduce_right(jnp.where(live, right, 0.0), y_rest[0], y_strides)
-        gather_start("gy", y_ends[1], sweep, ends_right(g))
-        v_ym, v_yp = outer_values("gy", *y_ends, sweep)
+        gather_start("gy", y_ends[1], sweep, ends_right(g), sides[1])
+        if more:
+            wide = halo_out.shape[3]
+            spread = lambda row, n: jnp.broadcast_to(row[:, n : n + 1], (1, wide))
+            halo_fill(late, YM, (g[1:2],), 2)
+            halo_fill(late, YP, (g[-2:-1],), 2)
+            halo_fill(early, YM, (u[:1], u[1:2], spread(u_xm, 0), spread(u_xp, 0)))
+            halo_fill(
+                early, YP,
+                (u[-1:], u[-2:-1], spread(u_xm, cy - 1), spread(u_xp, cy - 1)),
+            )
+            halo_fill(early, XM, (u_t[1:2],))
+            halo_fill(early, XP, (u_t[-2:-1],))
+            for direction in (YM, YP):
+                halo_start(early, direction)
+                halo_start(late, direction)
+            g_t = g.T
+            halo_fill(late, XM, (g_t[:1], g_t[1:2]), 4)
+            halo_fill(late, XP, (g_t[-1:], g_t[-2:-1]), 4)
+            for direction in (XM, XP):
+                halo_start(early, direction)
+                halo_start(late, direction)
+        else:
+            out[0] = u
+        before, after, far = outer_values("gy", *y_ends, sweep, sides)
+        v_ym, v_yp = before[:1], after[:1]
         v = g + y_rest[1] * v_ym + y_rest[2] * v_yp
-        if sweep + 1 < PASSES:
-            late = early + 1
-            halo_fill(late, YM, (v[1:2],))
-            halo_fill(late, YP, (v[-2:-1],))
-            halo_start(late, YM)
-            halo_start(late, YP)
-            u_ym, u_ym2 = halo_wait(early, YM, 2)
-            u_yp, u_yp2 = halo_wait(early, YP, 2)
+        if more:
             v_t = v.T
-            for direction, near, next_, lane in ((XM, 0, 1, 0), (XP, cx - 1, cx - 2, cx - 1)):
-                rows = [
-                    u_t[near : near + 1], v_t[near : near + 1],
-                    u_t[next_ : next_ + 1], v_t[next_ : next_ + 1],
-                ] + [
-                    jnp.broadcast_to(row[:, lane : lane + 1], (1, halo_out.shape[3]))
-                    for row in (u_ym, v_ym, u_yp, v_yp)
-                ]
-                halo_fill(late, direction, rows)
-                halo_start(late, direction)
+            u_ym, u_ym2, *low = halo_wait(early, YM, 4)
+            u_yp, u_yp2, *high = halo_wait(early, YP, 4)
+            (u_xm2,) = halo_wait(early, XM, 1)
+            (u_xp2,) = halo_wait(early, XP, 1)
+            p_2, q_2, g_2 = halo_wait(late, YM, 3)
+            v_ym2 = jnp.where(has(YM), g_2 + p_2 * far[0][:1] + q_2 * v[:1], 0.0)
+            p_2, q_2, g_2 = halo_wait(late, YP, 3)
+            v_yp2 = jnp.where(has(YP), g_2 + p_2 * v[-1:] + q_2 * far[1][:1], 0.0)
+
+            def beside(direction, row, lanes):
+                p_1, q_1, p_2, q_2, g_1, g_2 = halo_wait(late, direction, 6)
+                lo, hi = (
+                    [jnp.where(has(direction), end[row : row + 1, n : n + 1], 0.0) for n in lanes]
+                    for end in (before, after)
+                )
+                near = g_1 + p_1 * lo[0] + q_1 * hi[0]
+                next_ = g_2 + p_2 * lo[1] + q_2 * hi[1]
+                return near, next_, lo[0], hi[0]
+
+            v_xm, v_xm2, mm_v, mp_v = beside(XM, 1, (cx - 1, cx - 2))
+            v_xp, v_xp2, pm_v, pp_v = beside(XP, 2, (0, 1))
+            mm, mp = (low[0], mm_v), (high[0], mp_v)
+            pm, pp = (low[1], pm_v), (high[1], pp_v)
     out[1] = v
     for sweep in range(PASSES):
         for name, ends in gathers:
             for k in range(1, sizes[name]):
                 ends_copy(name, ends, sweep, k, me[name]).wait_send()
+    for sweep in range(PASSES - 1):
+        for ends, sides in zip(y_ends, side_sems):
+            for side in (XM, XP):
+
+                @pl.when(has(side))
+                def _():
+                    for k in range(sizes["gy"]):
+                        side_copy(
+                            ends, sides, sweep, side, k, me["gy"], side ^ 1
+                        ).wait_send()
 
 
 def on_device(sizes, velocity, wind_stress, thickness, ice_mask, land_mask):
@@ -489,16 +581,17 @@
             pltpu.VMEM((slots, 4, 8, wide), f32),
             pltpu.VMEM((4, 2, wide), f32),
             pltpu.VMEM((4, 2, wide), f32),
-            pltpu.VMEM((PASSES, nx, 6, cy), f32),
-            pltpu.VMEM((PASSES, nx, 2, cy), f32),
-            pltpu.VMEM((PASSES, ny, 6, cx), f32),
-            pltpu.VMEM((PASSES, ny, 2, cx), f32),
+            pltpu.VMEM((PASSES, nx, 1, 6, cy), f32),
+            pltpu.VMEM((PASSES, nx, 1, 2, cy), f32),
+            pltpu.VMEM((PASSES, ny, 3, 6, cx), f32),
+            pltpu.VMEM((PASSES, ny, 3, 2, cx), f32),
             pltpu.VMEM((strides, 3, cy, cx), f32),
             pltpu.VMEM((4, cy, cx), f32),
             dma((slots, 4)), dma((slots, 4)), dma((4,)), dma((4,)),
         ]
         + [dma((PASSES, nx - 1))] * 4
-        + [dma((PASSES, ny - 1))] * 4,
+        + [dma((PASSES, ny - 1))] * 4
+        + [dma((PASSES, 2, ny))] * 4,
         compiler_params=pltpu.CompilerParams(collective_id=0, has_side_effects=True),
         name="ice_relaxation",
     )(*args)

time: 28.7 us -> 26.4 us (0.920)
  Pallas kernels: 27.9 us -> 25.6 us
    pallas_call x1, Pallas kernels: 27.9 us -> 25.6 us  [on_device(): pl.pallas_call(functools.partial(kernel, sizes), out_shape=pltpu.VMEM(vel...]
where the time goes in v3:
time: 26.4 us; the launch traced here: 26.3 us
  Pallas kernels  25.6 us (97%)
  local copies, waits for them, and re-layouts  0.66 us (2%)
    pallas_call x1, Pallas kernels, on_device(): pl.pallas_call(functools.partial(kernel, sizes), out_shape=pltpu.VMEM(vel...  25.6 us
    unnamed x1, local copies, waits for them, and re-layouts  0.66 us

profile of v3, /device:TPU:0, one launch (start us, length us, event | category | flops | bytes accessed | tf_op | source)
XLA Modules:
  0.0 26.3 jit_solution(17747092109068714394)
XLA Ops:
  0.0 25.6 %ice_relaxation.1 = f32[2,128,128]{2,1,0:T(8,128)S(1)} custom-call(f32[2,128,128]{2,1,0:T(8,128)} %velocity_hbm.1, f32[2,128,128]{2,1,0:T(8,128)} %wind_hbm.1, f32[128,128]{1,0:T(8,128)} %thickness_hbm.1, s32[128,128]{1,0:T(8,128)} %ice_hbm.1, s32[128,128]{1,0:T(8,128)} %land_hbm.1), custom_call_target="tpu_custom_call" | custom-call | tf_op jit(solution)/shard_map/ice_relaxation/pallas_call | solution.py:572
  25.6 0.7 %copy.7 = f32[2,128,128]{2,1,0:T(8,128)} copy(f32[2,128,128]{2,1,0:T(8,128)S(1)} %ice_relaxation.1) | data formatting | bytes 262144

commit v4 on v3

--- a/solution.py
+++ b/solution.py
@@ -276,7 +276,8 @@
 
     def gather_start(name, ends, sweep, block, sides=None):
         ends[0][sweep, me[name], 0] = block
-        for k in range(1, sizes[name]):
+        half = sizes[name] // 2
+        for k in sorted(range(1, sizes[name]), key=lambda k: abs(k - half)):
             ends_copy(name, ends, sweep, k, me[name]).start()
         if sides is not None:
             for side in (XM, XP):

time: 26.4 us -> 26.5 us (level)
  no operation moved by 1% of the time
where the time goes in v4:
time: 26.5 us; the launch traced here: 26.3 us
  Pallas kernels  25.7 us (97%)
  local copies, waits for them, and re-layouts  0.66 us (2%)
    pallas_call x1, Pallas kernels, on_device(): pl.pallas_call(functools.partial(kernel, sizes), out_shape=pltpu.VMEM(vel...  25.7 us
    unnamed x1, local copies, waits for them, and re-layouts  0.66 us

profile of v4, /device:TPU:0, one launch (start us, length us, event | category | flops | bytes accessed | tf_op | source)
XLA Modules:
  0.0 26.3 jit_solution(12760672253545482105)
XLA Ops:
  0.0 25.7 %ice_relaxation.1 = f32[2,128,128]{2,1,0:T(8,128)S(1)} custom-call(f32[2,128,128]{2,1,0:T(8,128)} %velocity_hbm.1, f32[2,128,128]{2,1,0:T(8,128)} %wind_hbm.1, f32[128,128]{1,0:T(8,128)} %thickness_hbm.1, s32[128,128]{1,0:T(8,128)} %ice_hbm.1, s32[128,128]{1,0:T(8,128)} %land_hbm.1), custom_call_target="tpu_custom_call" | custom-call | tf_op jit(solution)/shard_map/ice_relaxation/pallas_call | solution.py:573
  25.7 0.7 %copy.7 = f32[2,128,128]{2,1,0:T(8,128)} copy(f32[2,128,128]{2,1,0:T(8,128)S(1)} %ice_relaxation.1) | data formatting | bytes 262144
